TPU v7x, 32 devices: a whole 2x2x4 slice. The times are simulated.
32 devices in a mesh: gx: 8 (over y, x, core), gy: 4 (over z).
Axes of the slice: x: 2, y: 2, z: 4, core: 2. Of those that a mesh axis runs over, the one named last changes fastest.
Arguments:
- panel: bfloat16 [8, 4, 2, 128, 1024], P('gx', 'gy'), may hold values from -0.5 to 0.5
- corner_panel: bfloat16 [8, 4, 2, 24, 128], P('gx', 'gy'), may hold values from -0.5 to 0.5
- interface_diag: float32 [8, 4, 2, 1024], P('gx', 'gy'), may hold values from 0.5 to 2
- coarse_diag: float32 [8, 128], P('gx'), may hold values from 0.5 to 2
- scaling: float32 [8, 4, 8, 128], P('gx', 'gy'), may hold values from 0.5 to 2
- dual_rhs: float32 [8, 4, 8, 128], P('gx', 'gy'), may hold values from -6 to 6
- block_map: int32 [8, 4, 2, 8], P('gx', 'gy'), may hold values from 0 to 39
- corner_map: int32 [8, 4, 2, 24], P('gx', 'gy'), may hold values from 0 to 127
- counts: int32 [8, 4], P('gx', 'gy'), may hold values from 1 to 2, as said below
Outputs:
- multipliers: float32 [8, 4, 8, 128], P('gx', 'gy')
- residual: float32 [8, 4, 8, 128], P('gx', 'gy')
Inputs may be any that keep to these rules, and one draw needn't show every extreme that they name: `counts`: every device holds one or more live subdomains in its first slots; some device has all 2 slots live and some has one.
All inputs are finite; a program needn't handle non-finite values.
Results may differ from a plain program's by a relative error of at most 0.0003.
Values sent between devices are 32-bit elements; how exact they have to be, the bound alone decides.
A program may use at most 64 MiB of HBM per device.

v0:
```python
import jax
import jax.numpy as jnp
from jax import lax
from jax.sharding import PartitionSpec as P

ITERS = 3


def extended(block, sides, width):
    for axis, dim in sides:
        count = lax.axis_size(axis)
        forward = [(i, i + 1) for i in range(count - 1)]
        backward = [(target, source) for source, target in forward]
        low = lax.ppermute(
            lax.slice_in_dim(block, block.shape[dim] - width, None, axis=dim), axis, forward
        )
        high = lax.ppermute(lax.slice_in_dim(block, 0, width, axis=dim), axis, backward)
        block = jnp.concatenate([low, block, high], axis=dim)
    return block


def weighted_norm(residual, precond):
    return lax.psum(jnp.sum(residual * precond), ("gx", "gy"))


def shards(
    panel,
    corner_panel,
    interface_diag,
    coarse_diag,
    scaling,
    dual_rhs,
    block_map,
    corner_map,
    counts,
):
    highest = lax.Precision.HIGHEST
    slots = panel.shape[2]
    width = panel.shape[4]
    owned = scaling.shape[2]
    block_size = scaling.shape[3]
    blocks_sub = width // block_size
    coarse_size = coarse_diag.shape[1]
    live = (lax.iota(jnp.int32, slots) < counts[0, 0]).astype(jnp.float32)
    factors = panel[0, 0]
    corners = corner_panel[0, 0]
    schur = jnp.einsum("sni,snj->sij", factors, factors, preferred_element_type=jnp.float32)
    width_eye = (lax.iota(jnp.int32, width)[:, None] == lax.iota(jnp.int32, width)[None, :]).astype(
        jnp.float32
    )
    schur = schur + interface_diag[0, 0][:, :, None] * width_eye[None]
    coupling = jnp.einsum("scn,sni->sci", corners, factors, preferred_element_type=jnp.float32)
    corner_block = (
        jnp.einsum("scn,sdn->scd", corners, corners, preferred_element_type=jnp.float32)
        * live[:, None, None]
    )
    local_map = block_map[0, 0]
    signs = jnp.where(local_map < owned, 1.0, -1.0) * live[:, None]
    picker = (local_map[:, :, None] == lax.iota(jnp.int32, 5 * owned)[None, None, :]).astype(
        jnp.float32
    ) * signs[:, :, None]
    coarse_iota = lax.iota(jnp.int32, coarse_size)
    own_hot = (corner_map[0, 0][:, :, None] == coarse_iota[None, None, :]).astype(jnp.float32)
    spread = jnp.einsum("sco,scd->sod", own_hot, corner_block, precision=highest)
    assembled = lax.psum(jnp.einsum("sod,sdp->op", spread, own_hot, precision=highest), "gy")
    coarse_eye = (coarse_iota[:, None] == coarse_iota[None, :]).astype(jnp.float32)
    system = assembled + coarse_diag[0][:, None] * coarse_eye
    lower = jnp.linalg.cholesky(system)

    def operate(field):
        padded = extended(field, (("gx", 0), ("gy", 1)), 1)
        candidates = jnp.concatenate(
            [padded[1, 1], padded[2, 1], padded[0, 1], padded[1, 2], padded[1, 0]], axis=0
        )
        gathered = jnp.einsum("sbk,kc->sbc", picker, candidates, precision=highest).reshape(
            slots, width
        )
        result = jnp.einsum("sij,sj->si", schur, gathered, precision=highest)
        corner_values = (
            jnp.einsum("sci,si->sc", coupling, gathered, precision=highest) * live[:, None]
        )
        coarse_right = lax.psum(
            jnp.einsum("sco,sc->o", own_hot, corner_values, precision=highest), "gy"
        )
        coarse_sol = jax.scipy.linalg.cho_solve((lower, True), coarse_right)
        back_values = jnp.einsum("sco,o->sc", own_hot, coarse_sol, precision=highest)
        result = result + jnp.einsum("sci,sc->si", coupling, back_values, precision=highest)
        contrib = jnp.einsum(
            "sbk,sbc->kc", picker, result.reshape(slots, blocks_sub, block_size), precision=highest
        )
        outgoing = contrib[owned:].reshape(4, owned, block_size)[None, None]
        incoming = extended(outgoing, (("gx", 0), ("gy", 1)), 1)
        image = field[0, 0] + contrib[:owned]
        image = (
            image + incoming[0, 1, 0] + incoming[2, 1, 1] + incoming[1, 0, 2] + incoming[1, 2, 3]
        )
        return image[None, None]

    multipliers = jnp.zeros_like(dual_rhs)
    residual = dual_rhs
    direction = scaling * residual
    norm_now = weighted_norm(residual, direction)
    for sweep_index in range(ITERS):
        image = operate(direction)
        alpha = norm_now / lax.psum(jnp.sum(direction * image), ("gx", "gy"))
        multipliers = multipliers + alpha * direction
        residual = dual_rhs - operate(multipliers)
        precond = scaling * residual
        norm_next = weighted_norm(residual, precond)
        direction = precond + norm_next / norm_now * direction
        norm_now = norm_next
    return (multipliers, residual)


def solution(mesh):
    return jax.shard_map(
        shards,
        mesh=mesh,
        in_specs=(
            P("gx", "gy", None, None, None),
            P("gx", "gy", None, None, None),
            P("gx", "gy", None, None),
            P("gx", None),
            P("gx", "gy", None, None),
            P("gx", "gy", None, None),
            P("gx", "gy", None, None),
            P("gx", "gy", None, None),
            P("gx", "gy"),
        ),
        out_specs=(P("gx", "gy", None, None), P("gx", "gy", None, None)),
        check_vma=False,
    )
```

profile of v0, /device:TPU:12, one launch (start us, length us, event | category | flops | bytes accessed | tf_op | source)
XLA Modules:
  0.0 578.4 jit_solution(1581443055216114433)
XLA Ops:
  9.9 4.5 collective-permute-start
  22.3 3.6 collective-permute-start.3
  32.1 7.2 %fusion.171 = f32[2,1,1024]{2,1,0:T(1,128)S(1)} fusion(f32[2,1024,1024]{2,1,0:T(8,128)S(1)} %multiply_add_fusion, f32[2,1024,1]{1,2,0:T(1,128)S(1)} %bitcast.652), kind=kOutput, calls=%fused_computation.326 | convolution fusion | flops 25165824 | bytes 8404992 | tf_op jit(solution)/shard_map/sij,sj->si/dot_general | solution.py:78
  39.5 9.2 %psum.93 = f32[128]{0:T(128)S(1)} all-reduce(f32[128]{0:T(128)S(1)} %convolution_bitcast_fusion.30), channel_id=1, replica_groups=mesh['gx'=8,'gy'=4] {'gy'}, use_global_device_ids=true, to_apply=%region_5.6 | all-reduce | flops 128 | bytes 1024 | tf_op jit(solution)/shard_map/psum | solution.py:82
  48.7 4.5 all-reduce.3.cloned.1.call-done
  55.2 11.7 %cholesky.19 = f32[128,128]{1,0:T(8,128)S(1)} custom-call(f32[128,128]{1,0:T(8,128)S(1)} %fusion.17), custom_call_target="Cholesky" | custom-call | tf_op jit(solution)/shard_map/jit(cholesky)/cholesky | solution.py:68
  68.2 9.8 %custom-call.13 = f32[1,128,128]{1,2,0:T(8,128)S(1)} custom-call(f32[1,128,128]{2,1,0:T(8,128)S(1)} %fusion.4), custom_call_target="InvertDiagBlocksLowerTriangular" | custom-call | tf_op jit(solution)/shard_map/jit(_cho_solve)/triangular_solve | solution.py:85
  83.6 3.5 collective-permute-done.4
  96.4 40.0 %all-reduce = (f32[]{:T(128)}, f32[]{:T(128)}) all-reduce(f32[]{:T(128)} %get-tuple-element.4, f32[]{:T(128)} %get-tuple-element.3), channel_id=1, replica_groups=mesh['gx'=8,'gy'=4] {'gx','gy'}, use_global_device_ids=true, to_apply=%region_1.2 | all-reduce | flops 2 | bytes 16 | tf_op jit(solution)/shard_map/psum | solution.py:23
  139.7 4.5 collective-permute-start.8
  155.0 9.4 %fusion.174 = f32[2,1,1024]{2,1,0:T(1,128)S(1)} fusion(f32[2,1024,1024]{2,1,0:T(8,128)} %copy-done.1, f32[2,1024,1]{1,2,0:T(1,128)S(1)} %bitcast.656), kind=kOutput, calls=%fused_computation.329 | convolution fusion | flops 25165824 | bytes 8404992 | tf_op jit(solution)/shard_map/sij,sj->si/dot_general | solution.py:78
  164.7 8.9 %psum.95 = f32[128]{0:T(128)S(1)} all-reduce(f32[128]{0:T(128)S(1)} %convolution_bitcast_fusion.29), channel_id=1, replica_groups=mesh['gx'=8,'gy'=4] {'gy'}, use_global_device_ids=true, to_apply=%region_8.10 | all-reduce | flops 128 | bytes 1024 | tf_op jit(solution)/shard_map/psum | solution.py:82
  179.2 3.5 collective-permute-done.12
  192.6 38.5 %psum.96 = f32[]{:T(128)} all-reduce(f32[]{:T(128)} %get-tuple-element.17), channel_id=1, replica_groups=mesh['gx'=8,'gy'=4] {'gx','gy'}, use_global_device_ids=true, to_apply=%region_10.12 | all-reduce | flops 1 | bytes 8 | tf_op jit(solution)/shard_map/psum | solution.py:23
  234.5 4.5 collective-permute-start.16
  249.1 9.4 %fusion.177 = f32[2,1,1024]{2,1,0:T(1,128)S(1)} fusion(f32[2,1024,1024]{2,1,0:T(8,128)} %copy-done.1, f32[2,1024,1]{1,2,0:T(1,128)S(1)} %bitcast.658), kind=kOutput, calls=%fused_computation.332 | convolution fusion | flops 25165824 | bytes 8404992 | tf_op jit(solution)/shard_map/sij,sj->si/dot_general | solution.py:78
  258.8 9.6 %psum.97 = f32[128]{0:T(128)S(1)} all-reduce(f32[128]{0:T(128)S(1)} %convolution_bitcast_fusion.28), channel_id=1, replica_groups=mesh['gx'=8,'gy'=4] {'gy'}, use_global_device_ids=true, to_apply=%region_11.13 | all-reduce | flops 128 | bytes 1024 | tf_op jit(solution)/shard_map/psum | solution.py:82
  273.9 3.5 collective-permute-done.20
  287.4 38.4 %psum.98 = f32[]{:T(128)} all-reduce(f32[]{:T(128)} %fusion.99), channel_id=1, replica_groups=mesh['gx'=8,'gy'=4] {'gx','gy'}, use_global_device_ids=true, to_apply=%region_13.15 | all-reduce | flops 1 | bytes 8 | tf_op jit(solution)/shard_map/psum | solution.py:105
  329.1 4.5 collective-permute-start.24
  343.7 9.4 %fusion.180 = f32[2,1,1024]{2,1,0:T(1,128)S(1)} fusion(f32[2,1024,1024]{2,1,0:T(8,128)} %copy-done.1, f32[2,1024,1]{1,2,0:T(1,128)S(1)} %bitcast.660), kind=kOutput, calls=%fused_computation.335 | convolution fusion | flops 25165824 | bytes 8404992 | tf_op jit(solution)/shard_map/sij,sj->si/dot_general | solution.py:78
  353.4 9.5 %psum.99 = f32[128]{0:T(128)S(1)} all-reduce(f32[128]{0:T(128)S(1)} %convolution_bitcast_fusion.27), channel_id=1, replica_groups=mesh['gx'=8,'gy'=4] {'gy'}, use_global_device_ids=true, to_apply=%region_14.16 | all-reduce | flops 128 | bytes 1024 | tf_op jit(solution)/shard_map/psum | solution.py:82
  368.5 3.5 collective-permute-done.28
  382.0 38.3 %psum.100 = f32[]{:T(128)} all-reduce(f32[]{:T(128)} %get-tuple-element.11), channel_id=1, replica_groups=mesh['gx'=8,'gy'=4] {'gx','gy'}, use_global_device_ids=true, to_apply=%region_16.18 | all-reduce | flops 1 | bytes 8 | tf_op jit(solution)/shard_map/psum | solution.py:23
  423.6 4.5 collective-permute-start.32
  438.2 9.4 %fusion.183 = f32[2,1,1024]{2,1,0:T(1,128)S(1)} fusion(f32[2,1024,1024]{2,1,0:T(8,128)} %copy-done.1, f32[2,1024,1]{1,2,0:T(1,128)S(1)} %bitcast.662), kind=kOutput, calls=%fused_computation.338 | convolution fusion | flops 25165824 | bytes 8404992 | tf_op jit(solution)/shard_map/sij,sj->si/dot_general | solution.py:78
  447.9 9.6 %psum.101 = f32[128]{0:T(128)S(1)} all-reduce(f32[128]{0:T(128)S(1)} %convolution_bitcast_fusion.26), channel_id=1, replica_groups=mesh['gx'=8,'gy'=4] {'gy'}, use_global_device_ids=true, to_apply=%region_17.19 | all-reduce | flops 128 | bytes 1024 | tf_op jit(solution)/shard_map/psum | solution.py:82
  463.1 3.5 collective-permute-done.36
  476.5 38.4 %psum.102 = f32[]{:T(128)} all-reduce(f32[]{:T(128)} %fusion.86), channel_id=1, replica_groups=mesh['gx'=8,'gy'=4] {'gx','gy'}, use_global_device_ids=true, to_apply=%region_19.21 | all-reduce | flops 1 | bytes 8 | tf_op jit(solution)/shard_map/psum | solution.py:105
  518.2 4.5 collective-permute-start.40
  532.6 9.4 %fusion.186 = f32[2,1,1024]{2,1,0:T(1,128)S(1)} fusion(f32[2,1024,1024]{2,1,0:T(8,128)} %copy-done.1, f32[2,1024,1]{1,2,0:T(1,128)S(1)} %bitcast.653), kind=kOutput, calls=%fused_computation.341 | convolution fusion | flops 25165824 | bytes 8404992 | tf_op jit(solution)/shard_map/sij,sj->si/dot_general | solution.py:78
  542.6 9.5 %psum.103 = f32[128]{0:T(128)S(1)} all-reduce(f32[128]{0:T(128)S(1)} %convolution_bitcast_fusion.25), channel_id=1, replica_groups=mesh['gx'=8,'gy'=4] {'gy'}, use_global_device_ids=true, to_apply=%region_20.22 | all-reduce | flops 128 | bytes 1024 | tf_op jit(solution)/shard_map/psum | solution.py:82
  (230 shorter events, 176.7 us)
Async XLA Ops:
  7.2 46.0 %all-reduce.3.cloned.1.call-start = ((), (), s32[]{:S(2)}) async-start(), calls=%async_computation | async-start | bytes 131072 | tf_op jit(solution)/shard_map/psum | solution.py:65
  8.0 14.3 %collective-permute-start.1 = (f32[1,1,8,128]{3,2,1,0:T(8,128)S(1)}, f32[1,1,8,128]{3,2,1,0:T(8,128)S(1)}, u32[]{:S(2)}, u32[]{:S(2)}) collective-permute-start(f32[1,1,8,128]{3,2,1,0:T(8,128)S(1)} %get-tuple-element.22), channel_id=1, source_target_pairs={{0,4},{4,8},{8,12},{12,16},{16,20},{20,24},{24,28},{1,5},{5,9},{9,... | collective-permute-start | bytes 12296 | tf_op jit(solution)/shard_map/ppermute | solution.py:14
  9.9 12.4 %collective-permute-start = (f32[1,1,8,128]{3,2,1,0:T(8,128)S(1)}, f32[1,1,8,128]{3,2,1,0:T(8,128)S(1)}, u32[]{:S(2)}, u32[]{:S(2)}) collective-permute-start(f32[1,1,8,128]{3,2,1,0:T(8,128)S(1)} %get-tuple-element.22), channel_id=1, source_target_pairs={{4,0},{8,4},{12,8},{16,12},{20,16},{24,20},{28,24},{5,1},{9,5},{13... | collective-permute-start | bytes 12296 | tf_op jit(solution)/shard_map/ppermute | solution.py:17
  22.3 9.2 %collective-permute-start.3 = (f32[3,1,8,128]{3,2,1,0:T(8,128)S(1)}, f32[3,1,8,128]{3,2,1,0:T(8,128)S(1)}, u32[]{:S(2)}, u32[]{:S(2)}) collective-permute-start(f32[3,1,8,128]{3,2,1,0:T(8,128)S(1)} %pad_maximum_fusion.6), channel_id=1, source_target_pairs={{0,1},{1,2},{2,3},{4,5},{5,6},{6,7},{8,9},{9,10},{10,11},{12,13},{... | collective-permute-start | bytes 36872 | tf_op jit(solution)/shard_map/ppermute | solution.py:14
  81.2 6.0 %collective-permute-start.4 = (f32[1,1,4,8,128]{4,3,2,1,0:T(8,128)S(1)}, f32[1,1,4,8,128]{4,3,2,1,0:T(8,128)S(1)}, u32[]{:S(2)}, u32[]{:S(2)}) collective-permute-start(f32[1,1,4,8,128]{4,3,2,1,0:T(8,128)S(1)} %slice_bitcast_fusion.5), channel_id=1, source_target_pairs={{0,4},{4,8},{8,12},{12,16},{16,20},{20,24},{24,28},{1,5},{5,9},{9,... | collective-permute-start | bytes 49160 | tf_op jit(solution)/shard_map/ppermute | solution.py:14
  87.2 6.0 %collective-permute-start.7 = (f32[3,1,4,8,128]{4,3,2,1,0:T(8,128)S(1)}, f32[3,1,4,8,128]{4,3,2,1,0:T(8,128)S(1)}, u32[]{:S(2)}, u32[]{:S(2)}) collective-permute-start(f32[3,1,4,8,128]{4,3,2,1,0:T(8,128)S(1)} %pad_maximum_fusion), channel_id=1, source_target_pairs={{1,0},{2,1},{3,2},{5,4},{6,5},{7,6},{9,8},{10,9},{11,10},{13,12},{... | collective-permute-start | bytes 147464 | tf_op jit(solution)/shard_map/ppermute | solution.py:17
  89.8 6.0 %collective-permute-start.6 = (f32[3,1,4,8,128]{4,3,2,1,0:T(8,128)S(1)}, f32[3,1,4,8,128]{4,3,2,1,0:T(8,128)S(1)}, u32[]{:S(2)}, u32[]{:S(2)}) collective-permute-start(f32[3,1,4,8,128]{4,3,2,1,0:T(8,128)S(1)} %pad_maximum_fusion), channel_id=1, source_target_pairs={{0,1},{1,2},{2,3},{4,5},{5,6},{6,7},{8,9},{9,10},{10,11},{12,13},{... | collective-permute-start | bytes 147464 | tf_op jit(solution)/shard_map/ppermute | solution.py:14
  137.8 6.5 %collective-permute-start.9 = (f32[1,1,8,128]{3,2,1,0:T(8,128)S(1)}, f32[1,1,8,128]{3,2,1,0:T(8,128)S(1)}, u32[]{:S(2)}, u32[]{:S(2)}) collective-permute-start(f32[1,1,8,128]{3,2,1,0:T(8,128)S(1)} %get-tuple-element.20), channel_id=1, source_target_pairs={{0,4},{4,8},{8,12},{12,16},{16,20},{20,24},{24,28},{1,5},{5,9},{9,... | collective-permute-start | bytes 12296 | tf_op jit(solution)/shard_map/ppermute | solution.py:14
  145.6 8.9 %collective-permute-start.11 = (f32[3,1,8,128]{3,2,1,0:T(8,128)S(1)}, f32[3,1,8,128]{3,2,1,0:T(8,128)S(1)}, u32[]{:S(2)}, u32[]{:S(2)}) collective-permute-start(f32[3,1,8,128]{3,2,1,0:T(8,128)S(1)} %pad_maximum_fusion.7), channel_id=1, source_target_pairs={{0,1},{1,2},{2,3},{4,5},{5,6},{6,7},{8,9},{9,10},{10,11},{12,13},{... | collective-permute-start | bytes 36872 | tf_op jit(solution)/shard_map/ppermute | solution.py:14
  176.7 6.0 %collective-permute-start.12 = (f32[1,1,4,8,128]{4,3,2,1,0:T(8,128)S(1)}, f32[1,1,4,8,128]{4,3,2,1,0:T(8,128)S(1)}, u32[]{:S(2)}, u32[]{:S(2)}) collective-permute-start(f32[1,1,4,8,128]{4,3,2,1,0:T(8,128)S(1)} %slice_bitcast_fusion.4), channel_id=1, source_target_pairs={{0,4},{4,8},{8,12},{12,16},{16,20},{20,24},{24,28},{1,5},{5,9},{9,... | collective-permute-start | bytes 49160 | tf_op jit(solution)/shard_map/ppermute | solution.py:14
  182.7 6.0 %collective-permute-start.15 = (f32[3,1,4,8,128]{4,3,2,1,0:T(8,128)S(1)}, f32[3,1,4,8,128]{4,3,2,1,0:T(8,128)S(1)}, u32[]{:S(2)}, u32[]{:S(2)}) collective-permute-start(f32[3,1,4,8,128]{4,3,2,1,0:T(8,128)S(1)} %pad_maximum_fusion.1), channel_id=1, source_target_pairs={{1,0},{2,1},{3,2},{5,4},{6,5},{7,6},{9,8},{10,9},{11,10},{13,12},{... | collective-permute-start | bytes 147464 | tf_op jit(solution)/shard_map/ppermute | solution.py:17
  186.0 6.0 %collective-permute-start.14 = (f32[3,1,4,8,128]{4,3,2,1,0:T(8,128)S(1)}, f32[3,1,4,8,128]{4,3,2,1,0:T(8,128)S(1)}, u32[]{:S(2)}, u32[]{:S(2)}) collective-permute-start(f32[3,1,4,8,128]{4,3,2,1,0:T(8,128)S(1)} %pad_maximum_fusion.1), channel_id=1, source_target_pairs={{0,1},{1,2},{2,3},{4,5},{5,6},{6,7},{8,9},{9,10},{10,11},{12,13},{... | collective-permute-start | bytes 147464 | tf_op jit(solution)/shard_map/ppermute | solution.py:14
  232.5 6.5 %collective-permute-start.17 = (f32[1,1,8,128]{3,2,1,0:T(8,128)S(1)}, f32[1,1,8,128]{3,2,1,0:T(8,128)S(1)}, u32[]{:S(2)}, u32[]{:S(2)}) collective-permute-start(f32[1,1,8,128]{3,2,1,0:T(8,128)S(1)} %get-tuple-element.16), channel_id=1, source_target_pairs={{0,4},{4,8},{8,12},{12,16},{16,20},{20,24},{24,28},{1,5},{5,9},{9,... | collective-permute-start | bytes 12296 | tf_op jit(solution)/shard_map/ppermute | solution.py:14
  240.3 8.2 %collective-permute-start.19 = (f32[3,1,8,128]{3,2,1,0:T(8,128)S(1)}, f32[3,1,8,128]{3,2,1,0:T(8,128)S(1)}, u32[]{:S(2)}, u32[]{:S(2)}) collective-permute-start(f32[3,1,8,128]{3,2,1,0:T(8,128)S(1)} %pad_maximum_fusion.8), channel_id=1, source_target_pairs={{0,1},{1,2},{2,3},{4,5},{5,6},{6,7},{8,9},{9,10},{10,11},{12,13},{... | collective-permute-start | bytes 36872 | tf_op jit(solution)/shard_map/ppermute | solution.py:14
  271.5 6.0 %collective-permute-start.20 = (f32[1,1,4,8,128]{4,3,2,1,0:T(8,128)S(1)}, f32[1,1,4,8,128]{4,3,2,1,0:T(8,128)S(1)}, u32[]{:S(2)}, u32[]{:S(2)}) collective-permute-start(f32[1,1,4,8,128]{4,3,2,1,0:T(8,128)S(1)} %slice_bitcast_fusion.3), channel_id=1, source_target_pairs={{0,4},{4,8},{8,12},{12,16},{16,20},{20,24},{24,28},{1,5},{5,9},{9,... | collective-permute-start | bytes 49160 | tf_op jit(solution)/shard_map/ppermute | solution.py:14
  277.5 6.0 %collective-permute-start.23 = (f32[3,1,4,8,128]{4,3,2,1,0:T(8,128)S(1)}, f32[3,1,4,8,128]{4,3,2,1,0:T(8,128)S(1)}, u32[]{:S(2)}, u32[]{:S(2)}) collective-permute-start(f32[3,1,4,8,128]{4,3,2,1,0:T(8,128)S(1)} %pad_maximum_fusion.2), channel_id=1, source_target_pairs={{1,0},{2,1},{3,2},{5,4},{6,5},{7,6},{9,8},{10,9},{11,10},{13,12},{... | collective-permute-start | bytes 147464 | tf_op jit(solution)/shard_map/ppermute | solution.py:17
  280.8 6.0 %collective-permute-start.22 = (f32[3,1,4,8,128]{4,3,2,1,0:T(8,128)S(1)}, f32[3,1,4,8,128]{4,3,2,1,0:T(8,128)S(1)}, u32[]{:S(2)}, u32[]{:S(2)}) collective-permute-start(f32[3,1,4,8,128]{4,3,2,1,0:T(8,128)S(1)} %pad_maximum_fusion.2), channel_id=1, source_target_pairs={{0,1},{1,2},{2,3},{4,5},{5,6},{6,7},{8,9},{9,10},{10,11},{12,13},{... | collective-permute-start | bytes 147464 | tf_op jit(solution)/shard_map/ppermute | solution.py:14
  327.1 6.5 %collective-permute-start.25 = (f32[1,1,8,128]{3,2,1,0:T(8,128)S(1)}, f32[1,1,8,128]{3,2,1,0:T(8,128)S(1)}, u32[]{:S(2)}, u32[]{:S(2)}) collective-permute-start(f32[1,1,8,128]{3,2,1,0:T(8,128)S(1)} %get-tuple-element.14), channel_id=1, source_target_pairs={{0,4},{4,8},{8,12},{12,16},{16,20},{20,24},{24,28},{1,5},{5,9},{9,... | collective-permute-start | bytes 12296 | tf_op jit(solution)/shard_map/ppermute | solution.py:14
  334.9 8.3 %collective-permute-start.27 = (f32[3,1,8,128]{3,2,1,0:T(8,128)S(1)}, f32[3,1,8,128]{3,2,1,0:T(8,128)S(1)}, u32[]{:S(2)}, u32[]{:S(2)}) collective-permute-start(f32[3,1,8,128]{3,2,1,0:T(8,128)S(1)} %pad_maximum_fusion.9), channel_id=1, source_target_pairs={{0,1},{1,2},{2,3},{4,5},{5,6},{6,7},{8,9},{9,10},{10,11},{12,13},{... | collective-permute-start | bytes 36872 | tf_op jit(solution)/shard_map/ppermute | solution.py:14
  366.1 6.0 %collective-permute-start.28 = (f32[1,1,4,8,128]{4,3,2,1,0:T(8,128)S(1)}, f32[1,1,4,8,128]{4,3,2,1,0:T(8,128)S(1)}, u32[]{:S(2)}, u32[]{:S(2)}) collective-permute-start(f32[1,1,4,8,128]{4,3,2,1,0:T(8,128)S(1)} %slice_bitcast_fusion.2), channel_id=1, source_target_pairs={{0,4},{4,8},{8,12},{12,16},{16,20},{20,24},{24,28},{1,5},{5,9},{9,... | collective-permute-start | bytes 49160 | tf_op jit(solution)/shard_map/ppermute | solution.py:14
  372.1 6.0 %collective-permute-start.31 = (f32[3,1,4,8,128]{4,3,2,1,0:T(8,128)S(1)}, f32[3,1,4,8,128]{4,3,2,1,0:T(8,128)S(1)}, u32[]{:S(2)}, u32[]{:S(2)}) collective-permute-start(f32[3,1,4,8,128]{4,3,2,1,0:T(8,128)S(1)} %pad_maximum_fusion.3), channel_id=1, source_target_pairs={{1,0},{2,1},{3,2},{5,4},{6,5},{7,6},{9,8},{10,9},{11,10},{13,12},{... | collective-permute-start | bytes 147464 | tf_op jit(solution)/shard_map/ppermute | solution.py:17
  375.4 6.0 %collective-permute-start.30 = (f32[3,1,4,8,128]{4,3,2,1,0:T(8,128)S(1)}, f32[3,1,4,8,128]{4,3,2,1,0:T(8,128)S(1)}, u32[]{:S(2)}, u32[]{:S(2)}) collective-permute-start(f32[3,1,4,8,128]{4,3,2,1,0:T(8,128)S(1)} %pad_maximum_fusion.3), channel_id=1, source_target_pairs={{0,1},{1,2},{2,3},{4,5},{5,6},{6,7},{8,9},{9,10},{10,11},{12,13},{... | collective-permute-start | bytes 147464 | tf_op jit(solution)/shard_map/ppermute | solution.py:14
  421.7 6.5 %collective-permute-start.33 = (f32[1,1,8,128]{3,2,1,0:T(8,128)S(1)}, f32[1,1,8,128]{3,2,1,0:T(8,128)S(1)}, u32[]{:S(2)}, u32[]{:S(2)}) collective-permute-start(f32[1,1,8,128]{3,2,1,0:T(8,128)S(1)} %get-tuple-element.10), channel_id=1, source_target_pairs={{0,4},{4,8},{8,12},{12,16},{16,20},{20,24},{24,28},{1,5},{5,9},{9,... | collective-permute-start | bytes 12296 | tf_op jit(solution)/shard_map/ppermute | solution.py:14
  429.5 8.2 %collective-permute-start.35 = (f32[3,1,8,128]{3,2,1,0:T(8,128)S(1)}, f32[3,1,8,128]{3,2,1,0:T(8,128)S(1)}, u32[]{:S(2)}, u32[]{:S(2)}) collective-permute-start(f32[3,1,8,128]{3,2,1,0:T(8,128)S(1)} %pad_maximum_fusion.10), channel_id=1, source_target_pairs={{0,1},{1,2},{2,3},{4,5},{5,6},{6,7},{8,9},{9,10},{10,11},{12,13},{... | collective-permute-start | bytes 36872 | tf_op jit(solution)/shard_map/ppermute | solution.py:14
  460.6 6.0 %collective-permute-start.36 = (f32[1,1,4,8,128]{4,3,2,1,0:T(8,128)S(1)}, f32[1,1,4,8,128]{4,3,2,1,0:T(8,128)S(1)}, u32[]{:S(2)}, u32[]{:S(2)}) collective-permute-start(f32[1,1,4,8,128]{4,3,2,1,0:T(8,128)S(1)} %slice_bitcast_fusion.1), channel_id=1, source_target_pairs={{0,4},{4,8},{8,12},{12,16},{16,20},{20,24},{24,28},{1,5},{5,9},{9,... | collective-permute-start | bytes 49160 | tf_op jit(solution)/shard_map/ppermute | solution.py:14
  466.6 6.0 %collective-permute-start.39 = (f32[3,1,4,8,128]{4,3,2,1,0:T(8,128)S(1)}, f32[3,1,4,8,128]{4,3,2,1,0:T(8,128)S(1)}, u32[]{:S(2)}, u32[]{:S(2)}) collective-permute-start(f32[3,1,4,8,128]{4,3,2,1,0:T(8,128)S(1)} %pad_maximum_fusion.4), channel_id=1, source_target_pairs={{1,0},{2,1},{3,2},{5,4},{6,5},{7,6},{9,8},{10,9},{11,10},{13,12},{... | collective-permute-start | bytes 147464 | tf_op jit(solution)/shard_map/ppermute | solution.py:17
  469.9 6.0 %collective-permute-start.38 = (f32[3,1,4,8,128]{4,3,2,1,0:T(8,128)S(1)}, f32[3,1,4,8,128]{4,3,2,1,0:T(8,128)S(1)}, u32[]{:S(2)}, u32[]{:S(2)}) collective-permute-start(f32[3,1,4,8,128]{4,3,2,1,0:T(8,128)S(1)} %pad_maximum_fusion.4), channel_id=1, source_target_pairs={{0,1},{1,2},{2,3},{4,5},{5,6},{6,7},{8,9},{9,10},{10,11},{12,13},{... | collective-permute-start | bytes 147464 | tf_op jit(solution)/shard_map/ppermute | solution.py:14
  516.3 6.5 %collective-permute-start.41 = (f32[1,1,8,128]{3,2,1,0:T(8,128)S(1)}, f32[1,1,8,128]{3,2,1,0:T(8,128)S(1)}, u32[]{:S(2)}, u32[]{:S(2)}) collective-permute-start(f32[1,1,8,128]{3,2,1,0:T(8,128)S(1)} %get-tuple-element.8), channel_id=1, source_target_pairs={{0,4},{4,8},{8,12},{12,16},{16,20},{20,24},{24,28},{1,5},{5,9},{9,... | collective-permute-start | bytes 12296 | tf_op jit(solution)/shard_map/ppermute | solution.py:14
  524.1 8.3 %collective-permute-start.43 = (f32[3,1,8,128]{3,2,1,0:T(8,128)S(1)}, f32[3,1,8,128]{3,2,1,0:T(8,128)S(1)}, u32[]{:S(2)}, u32[]{:S(2)}) collective-permute-start(f32[3,1,8,128]{3,2,1,0:T(8,128)S(1)} %pad_maximum_fusion.11), channel_id=1, source_target_pairs={{0,1},{1,2},{2,3},{4,5},{5,6},{6,7},{8,9},{9,10},{10,11},{12,13},{... | collective-permute-start | bytes 36872 | tf_op jit(solution)/shard_map/ppermute | solution.py:14
  555.2 6.0 %collective-permute-start.44 = (f32[1,1,4,8,128]{4,3,2,1,0:T(8,128)S(1)}, f32[1,1,4,8,128]{4,3,2,1,0:T(8,128)S(1)}, u32[]{:S(2)}, u32[]{:S(2)}) collective-permute-start(f32[1,1,4,8,128]{4,3,2,1,0:T(8,128)S(1)} %slice_bitcast_fusion), channel_id=1, source_target_pairs={{0,4},{4,8},{8,12},{12,16},{16,20},{20,24},{24,28},{1,5},{5,9},{9,... | collective-permute-start | bytes 49160 | tf_op jit(solution)/shard_map/ppermute | solution.py:14
  561.2 6.0 %collective-permute-start.47 = (f32[3,1,4,8,128]{4,3,2,1,0:T(8,128)S(1)}, f32[3,1,4,8,128]{4,3,2,1,0:T(8,128)S(1)}, u32[]{:S(2)}, u32[]{:S(2)}) collective-permute-start(f32[3,1,4,8,128]{4,3,2,1,0:T(8,128)S(1)} %pad_maximum_fusion.5), channel_id=1, source_target_pairs={{1,0},{2,1},{3,2},{5,4},{6,5},{7,6},{9,8},{10,9},{11,10},{13,12},{... | collective-permute-start | bytes 147464 | tf_op jit(solution)/shard_map/ppermute | solution.py:17
  564.5 6.0 %collective-permute-start.46 = (f32[3,1,4,8,128]{4,3,2,1,0:T(8,128)S(1)}, f32[3,1,4,8,128]{4,3,2,1,0:T(8,128)S(1)}, u32[]{:S(2)}, u32[]{:S(2)}) collective-permute-start(f32[3,1,4,8,128]{4,3,2,1,0:T(8,128)S(1)} %pad_maximum_fusion.5), channel_id=1, source_target_pairs={{0,1},{1,2},{2,3},{4,5},{5,6},{6,7},{8,9},{9,10},{10,11},{12,13},{... | collective-permute-start | bytes 147464 | tf_op jit(solution)/shard_map/ppermute | solution.py:14
  (25 other events, 449.8 us)
Sparse Core Ops, SparseCore 0:
  18.7 34.5 all-reduce.2
where the time goes:
time: 587 us; the launch traced here: 578 us
  blocking collectives  250 us (43%)
  starting transfers between devices  135 us (23%)
  matrix products  72.1 us (12%)
  waiting for transfers between devices  67.9 us (12%)
  other arithmetic  30.2 us (5%)
  between operations  22.8 us (4%)
    psum x3, blocking collectives, weighted_norm(): return lax.psum(jnp.sum(residual * precond), ('gx', 'gy'))  117 us
    psum x2, blocking collectives, shards(): alpha = norm_now / lax.psum(jnp.sum(direction * image), ('gx', 'gy'))  76.9 us
    ppermute x24, starting transfers between devices, extended(): lax.ppermute(lax.slice_in_dim(block, 0, width, axis=dim), axis, backward)  76.2 us
    ppermute x24, starting transfers between devices, extended(): lax.ppermute(lax.slice_in_dim(block, block.shape[dim] - width, None, axis...  58.9 us
    psum x6, blocking collectives, operate(): lax.psum(jnp.einsum('sco,sc->o', own_hot, corner_values, precision=highes...  56.3 us
    dot_general x6, matrix products, operate(): result = jnp.einsum('sij,sj->si', schur, gathered, precision=highest)  54.3 us
    ppermute x24, waiting for transfers between devices, extended(): lax.ppermute(lax.slice_in_dim(block, block.shape[dim] - width, None, axis...  40.6 us
    ppermute x24, waiting for transfers between devices, extended(): lax.ppermute(lax.slice_in_dim(block, 0, width, axis=dim), axis, backward)  22.8 us
  transfers between devices with their start and end apart: 49, of which 30 were waited for; matrix products, arithmetic and copies ran while one was open for 3% of the time, Pallas kernels for 0%

commit v1 on v0

v1 whole, which is shorter than its diff:
```python
import functools

import jax
import jax.numpy as jnp
from jax import lax
from jax.experimental import pallas as pl
from jax.experimental.pallas import tpu as pltpu
from jax.sharding import PartitionSpec as P

ITERS = 3
SCALE = 2.0**-8
MESH = pl.DeviceIdType.MESH
HIGHEST = lax.Precision.HIGHEST


def invert_tile(mat, tile):
    size = mat.shape[0]
    base = tile * 128
    if not isinstance(base, int):
        base = pl.multiple_of(base, 128)
    lanes = lax.broadcasted_iota(jnp.int32, (8, size), 1) - base
    subs = lax.broadcasted_iota(jnp.int32, (8, size), 0)
    narrow = lax.broadcasted_iota(jnp.int32, (8, 128), 0)
    for block in range(16):
        first = 8 * block
        rows = mat[pl.ds(base + first, 8), :]
        small = mat[pl.ds(base + first, 8), pl.ds(base, 128)]
        cols = [
            jnp.broadcast_to(small[:, first + c : first + c + 1], (8, 128)) for c in range(8)
        ]
        inside = (lanes >= first) & (lanes < first + 8)
        rows = jnp.where(inside, (lanes - first == subs).astype(jnp.float32), rows)
        for k in range(8):
            inverse = 1.0 / cols[k][k : k + 1, :]
            factor = cols[k]
            scaled = rows[k : k + 1, :] * jnp.tile(inverse, (1, size // 128))
            wide = jnp.tile(factor, (1, size // 128))
            rows = jnp.where(subs == k, scaled, rows - wide * scaled)
            for c in range(k + 1, 8):
                own = cols[c][k : k + 1, :] * inverse
                cols[c] = jnp.where(narrow == k, own, cols[c] - factor * own)

        def update(start, count):
            panel = mat[pl.ds(start, count), pl.ds(base, 128)]
            old = mat[pl.ds(start, count), :]
            total = jnp.where(inside[0:1, :], 0.0, old)
            for c in range(8):
                total = total - panel[:, first + c : first + c + 1] * rows[c : c + 1, :]
            mat[pl.ds(start, count), :] = total

        if size == 128:
            update(0, size)
        else:
            @pl.loop(0, size // 8)
            def _(chunk):
                update(pl.multiple_of(chunk * 8, 8), 8)

        mat[pl.ds(base + first, 8), :] = rows


def combine(moments):
    inverse_scale = 1.0 / SCALE
    res = [jnp.ones_like(moments[0])]
    direc = [jnp.ones_like(moments[0])]
    mult = []
    norm = moments[0]

    def form(left, right, shift):
        total = None
        for i, a in enumerate(left):
            for j, b in enumerate(right):
                term = a * b * moments[i + j + shift]
                total = term if total is None else total + term
        return total

    for step in range(ITERS):
        energy = form(direc, direc, 1) * inverse_scale
        alpha = norm / energy
        mult = [
            (mult[i] if i < len(mult) else 0.0) + alpha * direc[i] for i in range(len(direc))
        ]
        image = [None] + [d * inverse_scale for d in direc]
        res = [
            (res[i] if i < len(res) else 0.0)
            - (alpha * image[i] if image[i] is not None else 0.0)
            for i in range(len(image))
        ]
        if step < ITERS - 1:
            after = form(res, res, 0)
            beta = after / norm
            direc = [res[i] + (beta * direc[i] if i < len(direc) else 0.0) for i in range(len(res))]
            norm = after
    return mult, res


def kernel(
    nx,
    ny,
    block_map,
    counts,
    panel,
    corner,
    diag,
    coarse_diag,
    scaling,
    rhs,
    map_rows,
    corner_map,
    mult_out,
    res_out,
    cand,
    contrib,
    inbox,
    wide,
    pick,
    part,
    mat,
    expand,
    spread,
    gpart,
    red_x,
    red_y,
    halo_send,
    halo_recv,
    back_send,
    back_recv,
    mat_send,
    mat_recv,
    g_send,
    g_recv,
    rx_send,
    rx_recv,
    ry_send,
    ry_recv,
):
    slots, rows, width = panel.shape
    owned, lanes = scaling.shape
    per_sub = width // lanes
    coarse = coarse_diag.shape[1]
    x = lax.axis_index("gx")
    y = lax.axis_index("gy")

    cand[...] = jnp.zeros_like(cand)
    inbox[...] = jnp.zeros_like(inbox)

    barrier = pltpu.get_barrier_semaphore()
    for off in range(1, nx):
        pl.semaphore_signal(barrier, inc=1, device_id=(lax.rem(x + off, nx), y), device_id_type=MESH)
    for off in range(1, ny):
        pl.semaphore_signal(barrier, inc=1, device_id=(x, lax.rem(y + off, ny)), device_id_type=MESH)

    start = rhs[...]
    base_w = [start]
    base_y = [scaling[...] * start]
    cand[0, pl.ds(0, owned), :] = base_y[0]

    total = None
    for s in range(slots):
        live = jnp.where(counts[0, 0] > s, 1.0, 0.0)
        hot = lax.broadcasted_iota(jnp.int32, (coarse, corner.shape[1]), 0) == corner_map[s : s + 1, :]
        local = jnp.dot(
            hot.astype(jnp.float32).astype(jnp.bfloat16), corner[s], preferred_element_type=jnp.float32
        )
        local = local * live
        expand[s] = local.T
        term = lax.dot_general(
            local, local, (((1,), (1,)), ((), ())), precision=HIGHEST, preferred_element_type=jnp.float32
        )
        total = term if total is None else total + term
    part[0] = total

    pl.semaphore_wait(barrier, nx + ny - 2)

    sides = [
        (x < nx - 1, (x + 1, y)),
        (x > 0, (x - 1, y)),
        (y < ny - 1, (x, y + 1)),
        (y > 0, (x, y - 1)),
    ]
    opposite = [1, 0, 3, 2]

    def halo_copy(k, d):
        return pltpu.make_async_remote_copy(
            src_ref=cand.at[k, pl.ds(0, owned)],
            dst_ref=cand.at[k, pl.ds((1 + opposite[d]) * owned, owned)],
            send_sem=halo_send.at[k, d],
            recv_sem=halo_recv.at[k, opposite[d]],
            device_id=sides[d][1],
            device_id_type=MESH,
        )

    def back_copy(k, d):
        return pltpu.make_async_remote_copy(
            src_ref=contrib.at[k, d],
            dst_ref=inbox.at[k, opposite[d]],
            send_sem=back_send.at[k, d],
            recv_sem=back_recv.at[k, opposite[d]],
            device_id=sides[d][1],
            device_id_type=MESH,
        )

    def halo_arrival(k, d):
        return pltpu.make_async_remote_copy(
            src_ref=cand.at[k, pl.ds(0, owned)],
            dst_ref=cand.at[k, pl.ds((1 + d) * owned, owned)],
            send_sem=halo_send.at[k, d],
            recv_sem=halo_recv.at[k, d],
            device_id=sides[d][1],
            device_id_type=MESH,
        )

    def back_arrival(k, d):
        return pltpu.make_async_remote_copy(
            src_ref=contrib.at[k, d],
            dst_ref=inbox.at[k, d],
            send_sem=back_send.at[k, d],
            recv_sem=back_recv.at[k, d],
            device_id=sides[d][1],
            device_id_type=MESH,
        )

    def each_side(action):
        for d in range(4):
            @pl.when(sides[d][0])
            def _(d=d):
                action(d)

    def along_y(buf, off, send, recv):
        return pltpu.make_async_remote_copy(
            src_ref=buf.at[0],
            dst_ref=buf.at[off],
            send_sem=send.at[off],
            recv_sem=recv.at[off],
            device_id=(x, lax.rem(y + off, ny)),
            device_id_type=MESH,
        )

    def along_x(buf, off, send, recv):
        return pltpu.make_async_remote_copy(
            src_ref=buf.at[0],
            dst_ref=buf.at[off],
            send_sem=send.at[off],
            recv_sem=recv.at[off],
            device_id=(lax.rem(x + off, nx), y),
            device_id_type=MESH,
        )

    each_side(lambda d: halo_copy(0, d).start())
    mat_copies = [along_y(part, off, mat_send, mat_recv) for off in range(1, ny)]
    for copy in mat_copies:
        copy.start()

    for s in range(slots):
        wide[s] = panel[s].astype(jnp.float32)
    signs = []
    for s in range(slots):
        live = jnp.where(counts[0, 0] > s, 1.0, 0.0)
        here = map_rows[s : s + 1, :]
        sign_row = jnp.where(here < owned, live, -live)
        hit = lax.broadcasted_iota(jnp.int32, (5 * owned, per_sub), 0) == here
        table = jnp.where(hit, sign_row, 0.0)
        for b in range(per_sub):
            pick[s, b] = jnp.broadcast_to(table[:, b : b + 1], (5 * owned, lanes))
        signs.append([jnp.where(block_map[s, b] < owned, live, -live) for b in range(per_sub)])

    zero_y = jnp.where(y == 0, 1.0, 0.0)
    waits = []
    for k in range(ITERS):
        each_side(lambda d: halo_arrival(k, d).wait_recv())
        values, inner = [], []
        gsum = None
        for s in range(slots):
            held = [
                cand[k, pl.ds(block_map[s, b], 1), :] * signs[s][b] for b in range(per_sub)
            ]
            acc = None
            for b in range(per_sub):
                term = wide[s, :, b * lanes : (b + 1) * lanes] * held[b]
                acc = term if acc is None else acc + term
            col = jnp.sum(acc, axis=1, keepdims=True)
            term = jnp.sum(expand[s] * col, axis=0, keepdims=True)
            gsum = term if gsum is None else gsum + term
            values.append(held)
            inner.append(col)
        gbuf = gpart.at[k]
        gbuf[0] = gsum
        copies = [along_y(gbuf, off, g_send.at[k], g_recv.at[k]) for off in range(1, ny)]
        for copy in copies:
            copy.start()
        waits.extend(copies)
        if k == 0:
            for copy in mat_copies:
                copy.wait()
            full = part[0]
            for off in range(1, ny):
                full = full + part[off]
            eye = lax.broadcasted_iota(jnp.int32, (coarse, coarse), 0) == lax.broadcasted_iota(
                jnp.int32, (coarse, coarse), 1
            )
            mat[...] = full + jnp.where(eye, coarse_diag[...], 0.0)
            if coarse == 128:
                invert_tile(mat, 0)
            else:
                @pl.loop(0, coarse // 128)
                def _(tile):
                    invert_tile(mat, tile)
            for s in range(slots):
                spread[s] = jnp.dot(
                    expand[s], mat[...], precision=HIGHEST, preferred_element_type=jnp.float32
                )
        for copy in copies:
            copy.wait_recv()
        gall = gbuf[0]
        for off in range(1, ny):
            gall = gall + gbuf[off]
        total = None
        energy = None
        for s in range(slots):
            if k == ITERS - 1:
                more = jnp.sum(inner[s] * inner[s], axis=0, keepdims=True) * (1.0 / lanes)
                more = jnp.broadcast_to(more, (1, lanes))
                for b in range(per_sub):
                    more = more + diag[s : s + 1, b * lanes : (b + 1) * lanes] * (
                        values[s][b] * values[s][b]
                    )
                energy = more if energy is None else energy + more
            col = inner[s] + jnp.sum(spread[s] * gall, axis=1, keepdims=True)
            for b in range(per_sub):
                piece = jnp.sum(
                    wide[s, :, b * lanes : (b + 1) * lanes] * col, axis=0, keepdims=True
                )
                piece = piece + diag[s : s + 1, b * lanes : (b + 1) * lanes] * values[s][b]
                term = pick[s, b] * piece
                total = term if total is None else total + term
        for d in range(4):
            contrib[k, d] = total[(1 + d) * owned : (2 + d) * owned, :]
        each_side(lambda d: back_copy(k, d).start())
        image = base_y[k] + total[:owned, :]
        if k == ITERS - 1:
            sol = jnp.dot(
                jnp.broadcast_to(gall, (8, coarse)),
                mat[...],
                precision=HIGHEST,
                preferred_element_type=jnp.float32,
            )[0:1, :]
            work = gall * sol * zero_y
            for c in range(coarse // lanes):
                energy = energy + work[:, c * lanes : (c + 1) * lanes]
            energy = energy + jnp.sum(base_y[k] * base_y[k], axis=0, keepdims=True)
            moments = [
                jnp.sum(base_w[i // 2 + i % 2] * base_y[i // 2], axis=0, keepdims=True)
                for i in range(2 * ITERS - 1)
            ] + [energy * SCALE]
            for i in range(2 * ITERS):
                red_x[0, i : i + 1, :] = moments[i]
            x_copies = [along_x(red_x, off, rx_send, rx_recv) for off in range(1, nx)]
            for copy in x_copies:
                copy.start()
        each_side(lambda d: back_arrival(k, d).wait_recv())
        for d in range(4):
            image = image + inbox[k, d]
        base_w.append(image * SCALE)
        if k < ITERS - 1:
            base_y.append(scaling[...] * base_w[-1])
            cand[k + 1, pl.ds(0, owned), :] = base_y[-1]
            each_side(lambda d: halo_copy(k + 1, d).start())

    for copy in x_copies:
        copy.wait_recv()
    summed = red_x[0]
    for off in range(1, nx):
        summed = summed + red_x[off]
    red_y[0] = summed
    y_copies = [along_y(red_y, off, ry_send, ry_recv) for off in range(1, ny)]
    for copy in y_copies:
        copy.start()
    for copy in y_copies:
        copy.wait_recv()
    summed = red_y[0]
    for off in range(1, ny):
        summed = summed + red_y[off]
    summed = jnp.broadcast_to(jnp.sum(summed, axis=1, keepdims=True), summed.shape)
    mult, res = combine([summed[i : i + 1, :] for i in range(2 * ITERS)])
    out = base_y[0] * mult[0]
    for i in range(1, ITERS):
        out = out + base_y[i] * mult[i]
    mult_out[...] = out
    out = base_w[0] * res[0]
    for i in range(1, ITERS + 1):
        out = out + base_w[i] * res[i]
    res_out[...] = out

    for k in range(ITERS):
        each_side(lambda d: halo_copy(k, d).wait_send())
        each_side(lambda d: back_copy(k, d).wait_send())
    for copy in waits + x_copies + y_copies:
        copy.wait_send()


def shards(
    nx,
    ny,
    panel,
    corner_panel,
    interface_diag,
    coarse_diag,
    scaling,
    dual_rhs,
    block_map,
    corner_map,
    counts,
):
    slots, rows, width = panel.shape[2:]
    owned, lanes = scaling.shape[2:]
    per_sub = width // lanes
    coarse = coarse_diag.shape[1]
    vmem = pl.BlockSpec(memory_space=pltpu.VMEM)
    smem = pl.BlockSpec(memory_space=pltpu.SMEM)
    f32 = jnp.float32
    dma = pltpu.SemaphoreType.DMA
    out = jax.ShapeDtypeStruct((owned, lanes), f32)
    mult, res = pl.pallas_call(
        functools.partial(kernel, nx, ny),
        out_shape=(out, out),
        in_specs=[smem, smem] + [vmem] * 8,
        out_specs=(vmem, vmem),
        scratch_shapes=[
            pltpu.VMEM((ITERS, 5 * owned, lanes), f32),
            pltpu.VMEM((ITERS, 4, owned, lanes), f32),
            pltpu.VMEM((ITERS, 4, owned, lanes), f32),
            pltpu.VMEM((slots, rows, width), f32),
            pltpu.VMEM((slots, per_sub, 5 * owned, lanes), f32),
            pltpu.VMEM((ny, coarse, coarse), f32),
            pltpu.VMEM((coarse, coarse), f32),
            pltpu.VMEM((slots, rows, coarse), f32),
            pltpu.VMEM((slots, rows, coarse), f32),
            pltpu.VMEM((ITERS, ny, 1, coarse), f32),
            pltpu.VMEM((nx, 2 * ITERS, lanes), f32),
            pltpu.VMEM((ny, 2 * ITERS, lanes), f32),
            dma((ITERS, 4)),
            dma((ITERS, 4)),
            dma((ITERS, 4)),
            dma((ITERS, 4)),
            dma((ny,)),
            dma((ny,)),
            dma((ITERS, ny)),
            dma((ITERS, ny)),
            dma((nx,)),
            dma((nx,)),
            dma((ny,)),
            dma((ny,)),
        ],
        compiler_params=pltpu.CompilerParams(
            collective_id=0, has_side_effects=True, vmem_limit_bytes=56 * 2**20
        ),
    )(
        block_map[0, 0],
        counts,
        panel[0, 0],
        corner_panel[0, 0],
        interface_diag[0, 0],
        coarse_diag,
        scaling[0, 0],
        dual_rhs[0, 0],
        block_map[0, 0],
        corner_map[0, 0],
    )
    return mult[None, None], res[None, None]


def solution(mesh):
    nx, ny = mesh.shape["gx"], mesh.shape["gy"]
    return jax.shard_map(
        functools.partial(shards, nx, ny),
        mesh=mesh,
        in_specs=(
            P("gx", "gy", None, None, None),
            P("gx", "gy", None, None, None),
            P("gx", "gy", None, None),
            P("gx", None),
            P("gx", "gy", None, None),
            P("gx", "gy", None, None),
            P("gx", "gy", None, None),
            P("gx", "gy", None, None),
            P("gx", "gy"),
        ),
        out_specs=(P("gx", "gy", None, None), P("gx", "gy", None, None)),
        check_vma=False,
    )
```

time: 587 us -> 48.8 us (0.08)
  the two profiles are of different devices: /device:TPU:12 before, /device:TPU:0 now
where the time goes in v1:
time: 48.8 us; the launch traced here: 48.5 us
  Pallas kernels  45.3 us (93%)
  local copies, waits for them, and re-layouts  1.94 us (4%)
  between operations  1.3 us (3%)
    pallas_call x1, Pallas kernels, shards(): pl.pallas_call(functools.partial(kernel, nx, ny), out_shape=(out, out), i...  45.3 us
    unnamed x6, local copies, waits for them, and re-layouts  1.94 us

profile of v1, /device:TPU:0, one launch (start us, length us, event | category | flops | bytes accessed | tf_op | source)
XLA Modules:
  0.0 48.5 jit_solution(16560904962025051997)
XLA Ops:
  1.3 45.3 %shard_map.104 = (f32[8,128]{1,0:T(8,128)}, f32[8,128]{1,0:T(8,128)}) custom-call(s32[2,8]{1,0:T(2,128)} %bitcast.14, s32[1,1]{1,0:T(1,128)S(6)} %copy.13.counts, bf16[2,128,1024]{2,1,0:T(8,128)(2,1)} %bitcast.9, bf16[2,24,128]{2,1,0:T(8,128)(2,1)} %bitcast.10, f32[2,1024]{1,0:T(2,128)} %bitcast.11, f32[1,128]{1,0:T(1,128)} %coarse_diag.1, ...), custom_call_target="tpu_custom_call" | custom-call | tf_op jit(solution)/shard_map/pallas_call | solution.py:422
  46.6 0.0 copy-start.1
  46.6 0.7 %copy-done.1 = f32[8,128]{1,0:T(8,128)S(1)} copy-done((f32[8,128]{1,0:T(8,128)S(1)}, f32[8,128]{1,0:T(8,128)}, u32[]{:S(2)}) %copy-start.1) | copy-done | bytes 4120
  47.3 0.0 copy-start
  47.3 0.6 %copy.14 = f32[1,1,8,128]{3,2,1,0:T(8,128)} copy(f32[1,1,8,128]{3,2,1,0:T(8,128)S(1)} %bitcast.17) | data formatting | bytes 8192
  47.9 0.1 copy-done
  47.9 0.6 %copy.15 = f32[1,1,8,128]{3,2,1,0:T(8,128)} copy(f32[1,1,8,128]{3,2,1,0:T(8,128)S(1)} %bitcast.16) | data formatting | bytes 8192
Async XLA Ops:
  46.6 0.7 %copy-start.1 = (f32[8,128]{1,0:T(8,128)S(1)}, f32[8,128]{1,0:T(8,128)}, u32[]{:S(2)}) copy-start(f32[8,128]{1,0:T(8,128)} %get-tuple-element.4) | copy-start | bytes 12292
  47.3 0.7 %copy-start = (f32[8,128]{1,0:T(8,128)S(1)}, f32[8,128]{1,0:T(8,128)}, u32[]{:S(2)}) copy-start(f32[8,128]{1,0:T(8,128)} %get-tuple-element.5) | copy-start | bytes 12292

commit v2 on v1

--- a/solution.py
+++ b/solution.py
@@ -98,7 +98,7 @@
     ny,
     block_map,
     counts,
-    panel,
+    panel_hbm,
     corner,
     diag,
     coarse_diag,
@@ -119,7 +119,6 @@
     spread,
     gpart,
     red_x,
-    red_y,
     halo_send,
     halo_recv,
     back_send,
@@ -130,10 +129,12 @@
     g_recv,
     rx_send,
     rx_recv,
-    ry_send,
-    ry_recv,
+    panel,
+    load_sem,
 ):
     slots, rows, width = panel.shape
+    load = pltpu.make_async_copy(panel_hbm, panel, load_sem)
+    load.start()
     owned, lanes = scaling.shape
     per_sub = width // lanes
     coarse = coarse_diag.shape[1]
@@ -154,20 +155,25 @@
     base_y = [scaling[...] * start]
     cand[0, pl.ds(0, owned), :] = base_y[0]
 
-    total = None
+    ncor = corner.shape[1]
+    total_cor = slots * ncor
     for s in range(slots):
         live = jnp.where(counts[0, 0] > s, 1.0, 0.0)
-        hot = lax.broadcasted_iota(jnp.int32, (coarse, corner.shape[1]), 0) == corner_map[s : s + 1, :]
-        local = jnp.dot(
-            hot.astype(jnp.float32).astype(jnp.bfloat16), corner[s], preferred_element_type=jnp.float32
-        )
-        local = local * live
-        expand[s] = local.T
-        term = lax.dot_general(
-            local, local, (((1,), (1,)), ((), ())), precision=HIGHEST, preferred_element_type=jnp.float32
-        )
-        total = term if total is None else total + term
-    part[0] = total
+        hot = lax.broadcasted_iota(jnp.int32, (coarse, ncor), 0) == corner_map[s : s + 1, :]
+        gram = lax.dot_general(
+            corner[s], corner[s], (((1,), (1,)), ((), ())), preferred_element_type=jnp.float32
+        )
+        part[0, s * ncor : (s + 1) * ncor, :] = lax.dot_general(
+            gram * live,
+            hot.astype(jnp.float32),
+            (((1,), (1,)), ((), ())),
+            precision=HIGHEST,
+            preferred_element_type=jnp.float32,
+        )
+        for r in range(8):
+            part[0, total_cor + r : total_cor + r + 1, s * ncor : (s + 1) * ncor] = corner_map[
+                s : s + 1, :
+            ].astype(jnp.float32)
 
     pl.semaphore_wait(barrier, nx + ny - 2)
 
@@ -250,6 +256,15 @@
     for copy in mat_copies:
         copy.start()
 
+    for s in range(slots):
+        live = jnp.where(counts[0, 0] > s, 1.0, 0.0)
+        hot = lax.broadcasted_iota(jnp.int32, (coarse, ncor), 0) == corner_map[s : s + 1, :]
+        local = jnp.dot(
+            hot.astype(jnp.float32).astype(jnp.bfloat16), corner[s], preferred_element_type=jnp.float32
+        )
+        expand[s] = (local * live).T
+
+    load.wait()
     for s in range(slots):
         wide[s] = panel[s].astype(jnp.float32)
     signs = []
@@ -263,9 +278,13 @@
             pick[s, b] = jnp.broadcast_to(table[:, b : b + 1], (5 * owned, lanes))
         signs.append([jnp.where(block_map[s, b] < owned, live, -live) for b in range(per_sub)])
 
-    zero_y = jnp.where(y == 0, 1.0, 0.0)
     waits = []
     for k in range(ITERS):
+        if k == ITERS - 1:
+            known = [
+                jnp.sum(base_w[i // 2 + i % 2] * base_y[i // 2], axis=0, keepdims=True)
+                for i in range(2 * ITERS - 1)
+            ]
         each_side(lambda d: halo_arrival(k, d).wait_recv())
         values, inner = [], []
         gsum = None
@@ -283,17 +302,39 @@
             values.append(held)
             inner.append(col)
         gbuf = gpart.at[k]
-        gbuf[0] = gsum
+        if k < ITERS - 1:
+            gbuf[0] = jnp.broadcast_to(gsum, gbuf.shape[1:])
+        else:
+            energy = jnp.sum(base_y[k] * base_y[k], axis=0, keepdims=True)
+            for s in range(slots):
+                more = jnp.sum(inner[s] * inner[s], axis=0, keepdims=True) * (1.0 / lanes)
+                energy = energy + jnp.broadcast_to(more, (1, lanes))
+                for b in range(per_sub):
+                    energy = energy + diag[s : s + 1, b * lanes : (b + 1) * lanes] * (
+                        values[s][b] * values[s][b]
+                    )
+            gbuf[0] = jnp.broadcast_to(gsum, gbuf.shape[1:])
+            for i in range(2 * ITERS - 1):
+                gbuf[0, i + 1 : i + 2, 0:lanes] = known[i]
+            gbuf[0, 2 * ITERS : 2 * ITERS + 1, 0:lanes] = energy * SCALE
         copies = [along_y(gbuf, off, g_send.at[k], g_recv.at[k]) for off in range(1, ny)]
         for copy in copies:
             copy.start()
         waits.extend(copies)
         if k == 0:
             for copy in mat_copies:
-                copy.wait()
-            full = part[0]
-            for off in range(1, ny):
-                full = full + part[off]
+                copy.wait_recv()
+            waits.extend(mat_copies)
+            dofs = jnp.concatenate(
+                [part[off, total_cor : total_cor + 1, 0:total_cor] for off in range(ny)], axis=1
+            ).astype(jnp.int32)
+            all_hot = lax.broadcasted_iota(jnp.int32, (coarse, ny * total_cor), 0) == dofs
+            full = jnp.dot(
+                all_hot.astype(jnp.float32),
+                jnp.concatenate([part[off, 0:total_cor, :] for off in range(ny)], axis=0),
+                precision=HIGHEST,
+                preferred_element_type=jnp.float32,
+            )
             eye = lax.broadcasted_iota(jnp.int32, (coarse, coarse), 0) == lax.broadcasted_iota(
                 jnp.int32, (coarse, coarse), 1
             )
@@ -310,20 +351,12 @@
                 )
         for copy in copies:
             copy.wait_recv()
-        gall = gbuf[0]
+        gathered = gbuf[0]
         for off in range(1, ny):
-            gall = gall + gbuf[off]
+            gathered = gathered + gbuf[off]
+        gall = gathered[0:1, :]
         total = None
-        energy = None
         for s in range(slots):
-            if k == ITERS - 1:
-                more = jnp.sum(inner[s] * inner[s], axis=0, keepdims=True) * (1.0 / lanes)
-                more = jnp.broadcast_to(more, (1, lanes))
-                for b in range(per_sub):
-                    more = more + diag[s : s + 1, b * lanes : (b + 1) * lanes] * (
-                        values[s][b] * values[s][b]
-                    )
-                energy = more if energy is None else energy + more
             col = inner[s] + jnp.sum(spread[s] * gall, axis=1, keepdims=True)
             for b in range(per_sub):
                 piece = jnp.sum(
@@ -343,16 +376,12 @@
                 precision=HIGHEST,
                 preferred_element_type=jnp.float32,
             )[0:1, :]
-            work = gall * sol * zero_y
+            work = gall * sol
+            energy = gathered[2 * ITERS : 2 * ITERS + 1, 0:lanes]
             for c in range(coarse // lanes):
-                energy = energy + work[:, c * lanes : (c + 1) * lanes]
-            energy = energy + jnp.sum(base_y[k] * base_y[k], axis=0, keepdims=True)
-            moments = [
-                jnp.sum(base_w[i // 2 + i % 2] * base_y[i // 2], axis=0, keepdims=True)
-                for i in range(2 * ITERS - 1)
-            ] + [energy * SCALE]
-            for i in range(2 * ITERS):
-                red_x[0, i : i + 1, :] = moments[i]
+                energy = energy + work[:, c * lanes : (c + 1) * lanes] * SCALE
+            red_x[0] = gathered[1 : 2 * ITERS + 1, 0:lanes]
+            red_x[0, 2 * ITERS - 1 : 2 * ITERS, :] = energy
             x_copies = [along_x(red_x, off, rx_send, rx_recv) for off in range(1, nx)]
             for copy in x_copies:
                 copy.start()
@@ -370,15 +399,6 @@
     summed = red_x[0]
     for off in range(1, nx):
         summed = summed + red_x[off]
-    red_y[0] = summed
-    y_copies = [along_y(red_y, off, ry_send, ry_recv) for off in range(1, ny)]
-    for copy in y_copies:
-        copy.start()
-    for copy in y_copies:
-        copy.wait_recv()
-    summed = red_y[0]
-    for off in range(1, ny):
-        summed = summed + red_y[off]
     summed = jnp.broadcast_to(jnp.sum(summed, axis=1, keepdims=True), summed.shape)
     mult, res = combine([summed[i : i + 1, :] for i in range(2 * ITERS)])
     out = base_y[0] * mult[0]
@@ -393,7 +413,7 @@
     for k in range(ITERS):
         each_side(lambda d: halo_copy(k, d).wait_send())
         each_side(lambda d: back_copy(k, d).wait_send())
-    for copy in waits + x_copies + y_copies:
+    for copy in waits + x_copies:
         copy.wait_send()
 
 
@@ -414,6 +434,7 @@
     owned, lanes = scaling.shape[2:]
     per_sub = width // lanes
     coarse = coarse_diag.shape[1]
+    ncor = corner_panel.shape[3]
     vmem = pl.BlockSpec(memory_space=pltpu.VMEM)
     smem = pl.BlockSpec(memory_space=pltpu.SMEM)
     f32 = jnp.float32
@@ -422,7 +443,7 @@
     mult, res = pl.pallas_call(
         functools.partial(kernel, nx, ny),
         out_shape=(out, out),
-        in_specs=[smem, smem] + [vmem] * 8,
+        in_specs=[smem, smem, pl.BlockSpec(memory_space=pltpu.HBM)] + [vmem] * 7,
         out_specs=(vmem, vmem),
         scratch_shapes=[
             pltpu.VMEM((ITERS, 5 * owned, lanes), f32),
@@ -430,13 +451,12 @@
             pltpu.VMEM((ITERS, 4, owned, lanes), f32),
             pltpu.VMEM((slots, rows, width), f32),
             pltpu.VMEM((slots, per_sub, 5 * owned, lanes), f32),
-            pltpu.VMEM((ny, coarse, coarse), f32),
+            pltpu.VMEM((ny, slots * ncor + 8, coarse), f32),
             pltpu.VMEM((coarse, coarse), f32),
             pltpu.VMEM((slots, rows, coarse), f32),
             pltpu.VMEM((slots, rows, coarse), f32),
-            pltpu.VMEM((ITERS, ny, 1, coarse), f32),
+            pltpu.VMEM((ITERS, ny, 2 * ITERS + 2, coarse), f32),
             pltpu.VMEM((nx, 2 * ITERS, lanes), f32),
-            pltpu.VMEM((ny, 2 * ITERS, lanes), f32),
             dma((ITERS, 4)),
             dma((ITERS, 4)),
             dma((ITERS, 4)),
@@ -447,8 +467,8 @@
             dma((ITERS, ny)),
             dma((nx,)),
             dma((nx,)),
-            dma((ny,)),
-            dma((ny,)),
+            pltpu.VMEM((slots, rows, width), panel.dtype),
+            dma,
         ],
         compiler_params=pltpu.CompilerParams(
             collective_id=0, has_side_effects=True, vmem_limit_bytes=56 * 2**20

time: 48.8 us -> 42.2 us (0.86)
  Pallas kernels: 45.3 us -> 38.7 us
    pallas_call x1, Pallas kernels: 45.3 us -> 38.7 us  [shards(): pl.pallas_call(functools.partial(kernel, nx, ny), out_shape=(out, out), i...]
where the time goes in v2:
time: 42.2 us; the launch traced here: 42 us
  Pallas kernels  38.7 us (92%)
  local copies, waits for them, and re-layouts  1.94 us (5%)
  between operations  1.3 us (3%)
    pallas_call x1, Pallas kernels, shards(): pl.pallas_call(functools.partial(kernel, nx, ny), out_shape=(out, out), i...  38.7 us
    unnamed x6, local copies, waits for them, and re-layouts  1.94 us

profile of v2, /device:TPU:0, one launch (start us, length us, event | category | flops | bytes accessed | tf_op | source)
XLA Modules:
  0.0 42.0 jit_solution(8551948181956193390)
XLA Ops:
  1.3 38.7 %shard_map.104 = (f32[8,128]{1,0:T(8,128)}, f32[8,128]{1,0:T(8,128)}) custom-call(s32[2,8]{1,0:T(2,128)} %bitcast.14, s32[1,1]{1,0:T(1,128)S(6)} %copy.13.counts, bf16[2,128,1024]{2,1,0:T(8,128)(2,1)} %bitcast.9, bf16[2,24,128]{2,1,0:T(8,128)(2,1)} %bitcast.10, f32[2,1024]{1,0:T(2,128)} %bitcast.11, f32[1,128]{1,0:T(1,128)} %coarse_diag.1, ...), custom_call_target="tpu_custom_call" | custom-call | tf_op jit(solution)/shard_map/pallas_call | solution.py:443
  40.0 0.0 copy-start.1
  40.0 0.7 %copy-done.1 = f32[8,128]{1,0:T(8,128)S(1)} copy-done((f32[8,128]{1,0:T(8,128)S(1)}, f32[8,128]{1,0:T(8,128)}, u32[]{:S(2)}) %copy-start.1) | copy-done | bytes 4120
  40.7 0.0 copy-start
  40.7 0.6 %copy.14 = f32[1,1,8,128]{3,2,1,0:T(8,128)} copy(f32[1,1,8,128]{3,2,1,0:T(8,128)S(1)} %bitcast.17) | data formatting | bytes 8192
  41.3 0.1 copy-done
  41.4 0.6 %copy.15 = f32[1,1,8,128]{3,2,1,0:T(8,128)} copy(f32[1,1,8,128]{3,2,1,0:T(8,128)S(1)} %bitcast.16) | data formatting | bytes 8192
Async XLA Ops:
  40.0 0.7 %copy-start.1 = (f32[8,128]{1,0:T(8,128)S(1)}, f32[8,128]{1,0:T(8,128)}, u32[]{:S(2)}) copy-start(f32[8,128]{1,0:T(8,128)} %get-tuple-element.4) | copy-start | bytes 12292
  40.7 0.7 %copy-start = (f32[8,128]{1,0:T(8,128)S(1)}, f32[8,128]{1,0:T(8,128)}, u32[]{:S(2)}) copy-start(f32[8,128]{1,0:T(8,128)} %get-tuple-element.5) | copy-start | bytes 12292

commit v3 on v2

--- a/solution.py
+++ b/solution.py
@@ -117,6 +117,7 @@
     mat,
     expand,
     spread,
+    gfirst,
     gpart,
     red_x,
     halo_send,
@@ -141,9 +142,6 @@
     x = lax.axis_index("gx")
     y = lax.axis_index("gy")
 
-    cand[...] = jnp.zeros_like(cand)
-    inbox[...] = jnp.zeros_like(inbox)
-
     barrier = pltpu.get_barrier_semaphore()
     for off in range(1, nx):
         pl.semaphore_signal(barrier, inc=1, device_id=(lax.rem(x + off, nx), y), device_id_type=MESH)
@@ -177,31 +175,42 @@
 
     pl.semaphore_wait(barrier, nx + ny - 2)
 
+    low, high = y == 0, y == ny - 1
+    if nx % 2 == 0:
+        pair = x + 1 - 2 * lax.rem(x, 2)
+        up = (jnp.where(high, pair, x), jnp.where(high, y, y + 1))
+        down = (jnp.where(low, pair, x), jnp.where(low, y, y - 1))
+        up_slot, down_slot = jnp.where(high, 2, 3), jnp.where(low, 3, 2)
+    else:
+        up, down = (x, lax.rem(y + 1, ny)), (x, lax.rem(y + ny - 1, ny))
+        up_slot, down_slot = 3, 2
     sides = [
-        (x < nx - 1, (x + 1, y)),
-        (x > 0, (x - 1, y)),
-        (y < ny - 1, (x, y + 1)),
-        (y > 0, (x, y - 1)),
+        ((lax.rem(x + 1, nx), y), 1),
+        ((lax.rem(x + nx - 1, nx), y), 0),
+        (up, up_slot),
+        (down, down_slot),
     ]
-    opposite = [1, 0, 3, 2]
+    ones = [jnp.where(there, 1.0, 0.0) for there in (x < nx - 1, x > 0, y < ny - 1, y > 0)]
 
     def halo_copy(k, d):
+        peer, slot = sides[d]
         return pltpu.make_async_remote_copy(
             src_ref=cand.at[k, pl.ds(0, owned)],
-            dst_ref=cand.at[k, pl.ds((1 + opposite[d]) * owned, owned)],
+            dst_ref=cand.at[k, pl.ds((1 + slot) * owned, owned)],
             send_sem=halo_send.at[k, d],
-            recv_sem=halo_recv.at[k, opposite[d]],
-            device_id=sides[d][1],
+            recv_sem=halo_recv.at[k, slot],
+            device_id=peer,
             device_id_type=MESH,
         )
 
     def back_copy(k, d):
+        peer, slot = sides[d]
         return pltpu.make_async_remote_copy(
             src_ref=contrib.at[k, d],
-            dst_ref=inbox.at[k, opposite[d]],
+            dst_ref=inbox.at[k, slot],
             send_sem=back_send.at[k, d],
-            recv_sem=back_recv.at[k, opposite[d]],
-            device_id=sides[d][1],
+            recv_sem=back_recv.at[k, slot],
+            device_id=peer,
             device_id_type=MESH,
         )
 
@@ -211,7 +220,7 @@
             dst_ref=cand.at[k, pl.ds((1 + d) * owned, owned)],
             send_sem=halo_send.at[k, d],
             recv_sem=halo_recv.at[k, d],
-            device_id=sides[d][1],
+            device_id=sides[d][0],
             device_id_type=MESH,
         )
 
@@ -221,15 +230,20 @@
             dst_ref=inbox.at[k, d],
             send_sem=back_send.at[k, d],
             recv_sem=back_recv.at[k, d],
-            device_id=sides[d][1],
+            device_id=sides[d][0],
             device_id_type=MESH,
         )
 
     def each_side(action):
         for d in range(4):
-            @pl.when(sides[d][0])
-            def _(d=d):
-                action(d)
+            action(d)
+
+    def sign_of(target, live):
+        sign = jnp.where(target < owned, live, -live)
+        for d in range(4):
+            on_side = (target >= (1 + d) * owned) & (target < (2 + d) * owned)
+            sign = jnp.where(on_side, sign * ones[d], sign)
+        return sign
 
     def along_y(buf, off, send, recv):
         return pltpu.make_async_remote_copy(
@@ -271,12 +285,12 @@
     for s in range(slots):
         live = jnp.where(counts[0, 0] > s, 1.0, 0.0)
         here = map_rows[s : s + 1, :]
-        sign_row = jnp.where(here < owned, live, -live)
+        sign_row = sign_of(here, live)
         hit = lax.broadcasted_iota(jnp.int32, (5 * owned, per_sub), 0) == here
         table = jnp.where(hit, sign_row, 0.0)
         for b in range(per_sub):
             pick[s, b] = jnp.broadcast_to(table[:, b : b + 1], (5 * owned, lanes))
-        signs.append([jnp.where(block_map[s, b] < owned, live, -live) for b in range(per_sub)])
+        signs.append([sign_of(block_map[s, b], live) for b in range(per_sub)])
 
     waits = []
     for k in range(ITERS):
@@ -301,9 +315,9 @@
             gsum = term if gsum is None else gsum + term
             values.append(held)
             inner.append(col)
-        gbuf = gpart.at[k]
+        gbuf = gpart if k == ITERS - 1 else gfirst.at[k]
         if k < ITERS - 1:
-            gbuf[0] = jnp.broadcast_to(gsum, gbuf.shape[1:])
+            gbuf[0] = gsum
         else:
             energy = jnp.sum(base_y[k] * base_y[k], axis=0, keepdims=True)
             for s in range(slots):
@@ -455,7 +469,8 @@
             pltpu.VMEM((coarse, coarse), f32),
             pltpu.VMEM((slots, rows, coarse), f32),
             pltpu.VMEM((slots, rows, coarse), f32),
-            pltpu.VMEM((ITERS, ny, 2 * ITERS + 2, coarse), f32),
+            pltpu.VMEM((ITERS - 1, ny, 1, coarse), f32),
+            pltpu.VMEM((ny, 2 * ITERS + 2, coarse), f32),
             pltpu.VMEM((nx, 2 * ITERS, lanes), f32),
             dma((ITERS, 4)),
             dma((ITERS, 4)),

time: 42.2 us -> 41.8 us (level)
    pallas_call x1, Pallas kernels: 38.7 us -> 38.3 us  [shards(): pl.pallas_call(functools.partial(kernel, nx, ny), out_shape=(out, out), i...]
where the time goes in v3:
time: 41.8 us; the launch traced here: 41.5 us
  Pallas kernels  38.3 us (92%)
  local copies, waits for them, and re-layouts  1.94 us (5%)
  between operations  1.3 us (3%)
    pallas_call x1, Pallas kernels, shards(): pl.pallas_call(functools.partial(kernel, nx, ny), out_shape=(out, out), i...  38.3 us
    unnamed x6, local copies, waits for them, and re-layouts  1.94 us

profile of v3, /device:TPU:0, one launch (start us, length us, event | category | flops | bytes accessed | tf_op | source)
XLA Modules:
  0.0 41.5 jit_solution(10551934214840782009)
XLA Ops:
  1.3 38.3 %shard_map.104 = (f32[8,128]{1,0:T(8,128)}, f32[8,128]{1,0:T(8,128)}) custom-call(s32[2,8]{1,0:T(2,128)} %bitcast.14, s32[1,1]{1,0:T(1,128)S(6)} %copy.13.counts, bf16[2,128,1024]{2,1,0:T(8,128)(2,1)} %bitcast.9, bf16[2,24,128]{2,1,0:T(8,128)(2,1)} %bitcast.10, f32[2,1024]{1,0:T(2,128)} %bitcast.11, f32[1,128]{1,0:T(1,128)} %coarse_diag.1, ...), custom_call_target="tpu_custom_call" | custom-call | tf_op jit(solution)/shard_map/pallas_call | solution.py:457
  39.6 0.0 copy-start.1
  39.6 0.7 %copy-done.1 = f32[8,128]{1,0:T(8,128)S(1)} copy-done((f32[8,128]{1,0:T(8,128)S(1)}, f32[8,128]{1,0:T(8,128)}, u32[]{:S(2)}) %copy-start.1) | copy-done | bytes 4120
  40.2 0.0 copy-start
  40.2 0.6 %copy.14 = f32[1,1,8,128]{3,2,1,0:T(8,128)} copy(f32[1,1,8,128]{3,2,1,0:T(8,128)S(1)} %bitcast.17) | data formatting | bytes 8192
  40.8 0.1 copy-done
  40.9 0.6 %copy.15 = f32[1,1,8,128]{3,2,1,0:T(8,128)} copy(f32[1,1,8,128]{3,2,1,0:T(8,128)S(1)} %bitcast.16) | data formatting | bytes 8192
Async XLA Ops:
  39.6 0.7 %copy-start.1 = (f32[8,128]{1,0:T(8,128)S(1)}, f32[8,128]{1,0:T(8,128)}, u32[]{:S(2)}) copy-start(f32[8,128]{1,0:T(8,128)} %get-tuple-element.4) | copy-start | bytes 12292
  40.2 0.7 %copy-start = (f32[8,128]{1,0:T(8,128)S(1)}, f32[8,128]{1,0:T(8,128)}, u32[]{:S(2)}) copy-start(f32[8,128]{1,0:T(8,128)} %get-tuple-element.5) | copy-start | bytes 12292
